TPU v7x, 128 devices: a whole 4x4x4 slice. The times are simulated.
128 devices in a mesh: sx: 8 (over y, core), sy: 16 (over z, x).
Axes of the slice: x: 4, y: 4, z: 4, core: 2. Of those that a mesh axis runs over, the one named last changes fastest.
Arguments:
- features: bfloat16 [131072, 384], P(('sx', 'sy'))
- cotangent: bfloat16 [131072, 384], P(('sx', 'sy')), may hold values from -6 to 6
- hilbert_rank: int32 [131072], P(('sx', 'sy')), may hold values from 0 to 131071, as said below
- w_qkv: bfloat16 [384, 1152], replicated
- w_proj: bfloat16 [384, 384], replicated, may hold values from -0.3125 to 0.3125
Outputs:
- outputs: bfloat16 [131072, 384], P(('sx', 'sy'))
- grad_features: bfloat16 [131072, 384], P(('sx', 'sy'))
- grad_qkv: float32 [384, 1152], replicated
- grad_proj: float32 [384, 384], replicated
Inputs may be any that keep to these rules, and one draw needn't show every extreme that they name: hilbert_rank is a permutation. Hilbert positions t * 1024 to (t + 1) * 1024 - 1 belong to device t. Every device sends rows to every device, 4 to 16 rows to each, and every device has 16 rows for some owners and receives 16 rows from some devices.
All inputs are finite; a program needn't handle non-finite values.
Results may differ from a plain program's by a relative error of at most 0.004.
The roundings to bfloat16 on the way count: a program that leaves them out, or rounds other values in their place, can miss the bound.
Values may be sent and summed in bfloat16 or wider, within the bound.
A program may use at most 64 MiB of HBM per device.

v0:
```python
import math
import jax
import jax.numpy as jnp
from jax import lax
from jax.sharding import PartitionSpec as P

HEADS = 24
PATCH = 1024


def contract(left_op, right_op, left_dim, right_dim):
    return lax.dot_general(
        left_op,
        right_op,
        (((left_dim,), (right_dim,)), ((), ())),
        preferred_element_type=jnp.float32,
    )


def head_pass(query_rows, key_rows, value_rows, grad_slice):
    score_scale = query_rows.shape[1] ** (-0.5)
    scores = contract(query_rows, key_rows, 1, 1) * score_scale
    shifted = jnp.exp(scores - jnp.max(scores, axis=1, keepdims=True))
    prob_full = shifted / jnp.sum(shifted, axis=1, keepdims=True)
    prob_low = prob_full.astype(jnp.bfloat16)
    attended = jnp.dot(prob_low, value_rows, preferred_element_type=jnp.float32).astype(
        jnp.bfloat16
    )
    dprobs = contract(grad_slice, value_rows, 1, 1)
    dscores = (
        prob_full * (dprobs - jnp.sum(dprobs * prob_full, axis=1, keepdims=True)) * score_scale
    ).astype(jnp.bfloat16)
    dquery = jnp.dot(dscores, key_rows, preferred_element_type=jnp.float32).astype(jnp.bfloat16)
    dkey_rows = contract(dscores, query_rows, 0, 0).astype(jnp.bfloat16)
    dvalue = contract(prob_low, grad_slice, 0, 0).astype(jnp.bfloat16)
    return (attended, dquery, dkey_rows, dvalue)


def patch_pass(block_rows, block_grads, w_qkv, w_proj, head_count):
    feat_width = block_rows.shape[1]
    head_dim = feat_width // head_count
    values = block_rows.astype(jnp.float32)
    row_mean = jnp.mean(values, axis=1, keepdims=True)
    centred = values - row_mean
    inv_std = lax.rsqrt(jnp.mean(centred * centred, axis=1, keepdims=True) + 1e-05)
    normed = centred * inv_std
    normed_low = normed.astype(jnp.bfloat16)
    projected = jnp.dot(normed_low, w_qkv, preferred_element_type=jnp.float32).astype(jnp.bfloat16)
    upstream = contract(block_grads, w_proj, 1, 1).astype(jnp.bfloat16)

    def one_head(head_index):
        head_start = head_index * head_dim
        query_rows = lax.dynamic_slice_in_dim(projected, head_start, head_dim, 1)
        key_rows = lax.dynamic_slice_in_dim(projected, head_start + feat_width, head_dim, 1)
        value_rows = lax.dynamic_slice_in_dim(projected, head_start + 2 * feat_width, head_dim, 1)
        grad_slice = lax.dynamic_slice_in_dim(upstream, head_start, head_dim, 1)
        return head_pass(query_rows, key_rows, value_rows, grad_slice)

    heads_out = lax.map(one_head, jnp.arange(head_count, dtype=jnp.int32))

    def merge_heads(stacked):
        return jnp.transpose(stacked, (1, 0, 2)).reshape(stacked.shape[1], feat_width)

    attended = merge_heads(heads_out[0])
    dprojected = jnp.concatenate(
        [merge_heads(heads_out[1]), merge_heads(heads_out[2]), merge_heads(heads_out[3])], axis=1
    )
    mixed_out = jnp.dot(attended, w_proj, preferred_element_type=jnp.float32)
    output = (values + mixed_out).astype(jnp.bfloat16)
    dnormed = contract(dprojected, w_qkv, 1, 1)
    dnorm_mean = jnp.mean(dnormed, axis=1, keepdims=True)
    cross_mean = jnp.mean(dnormed * normed, axis=1, keepdims=True)
    dinput = inv_std * (dnormed - dnorm_mean - normed * cross_mean)
    grad_input = (block_grads.astype(jnp.float32) + dinput).astype(jnp.bfloat16)
    return (output, grad_input, normed_low, dprojected, attended)


def on_device(features, cotangent, hilbert_rank, w_qkv, w_proj):
    row_count = features.shape[0]
    feat_width = features.shape[1]
    size_x = lax.axis_size("sx")
    size_y = lax.axis_size("sy")
    devices = size_x * size_y
    capacity = 2 * row_count // devices
    slot_total = devices * capacity
    owner_dev = hilbert_rank // row_count
    place_row = hilbert_rank % row_count
    sort_order = jnp.argsort(hilbert_rank)
    owner_sorted = owner_dev[sort_order]
    labels = jnp.arange(devices, dtype=jnp.int32)
    counts = jnp.sum((owner_dev[:, None] == labels[None, :]).astype(jnp.int32), axis=0)
    starts = jnp.cumsum(counts) - counts
    first_slot = jnp.sum(
        jnp.where(owner_sorted[:, None] == labels[None, :], starts[None, :], 0), axis=1
    )
    slot_sorted = owner_sorted * capacity + jnp.arange(row_count, dtype=jnp.int32) - first_slot
    slot_index = jnp.zeros((row_count,), jnp.int32).at[sort_order].set(slot_sorted)
    send_rows = jnp.zeros((slot_total, feat_width), features.dtype).at[slot_index].set(features)
    send_grads = jnp.zeros((slot_total, feat_width), cotangent.dtype).at[slot_index].set(cotangent)
    send_place = jnp.full((slot_total,), row_count, jnp.int32).at[slot_index].set(place_row)
    got_rows, got_grads, got_place = (
        lax.all_to_all(send_rows, ("sx", "sy"), split_axis=0, concat_axis=0, tiled=True),
        lax.all_to_all(send_grads, ("sx", "sy"), split_axis=0, concat_axis=0, tiled=True),
        lax.all_to_all(send_place, ("sx", "sy"), split_axis=0, concat_axis=0, tiled=True),
    )
    curve_rows = (
        jnp.zeros((row_count, feat_width), jnp.bfloat16).at[got_place].set(got_rows, mode="drop")
    )
    curve_grads = (
        jnp.zeros((row_count, feat_width), jnp.bfloat16).at[got_place].set(got_grads, mode="drop")
    )
    patch_total = row_count // PATCH

    def run_patch(both_blocks):
        return patch_pass(both_blocks[0], both_blocks[1], w_qkv, w_proj, HEADS)

    results = lax.map(
        run_patch,
        (
            curve_rows.reshape(patch_total, PATCH, feat_width),
            curve_grads.reshape(patch_total, PATCH, feat_width),
        ),
    )
    curve_out = results[0].reshape(row_count, feat_width)
    curve_grad = results[1].reshape(row_count, feat_width)
    normed_low = results[2].reshape(row_count, feat_width)
    dprojected = results[3].reshape(row_count, 3 * feat_width)
    attended = results[4].reshape(row_count, feat_width)
    grad_terms = (contract(normed_low, dprojected, 0, 0), contract(attended, curve_grads, 0, 0))
    back_place = jnp.minimum(got_place, row_count - 1)
    back_rows = curve_out[back_place]
    back_grads = curve_grad[back_place]
    ret_rows, ret_grads = (
        lax.all_to_all(back_rows, ("sx", "sy"), split_axis=0, concat_axis=0, tiled=True),
        lax.all_to_all(back_grads, ("sx", "sy"), split_axis=0, concat_axis=0, tiled=True),
    )
    grad_sums = lax.psum((grad_terms[0], grad_terms[1]), ("sx", "sy"))
    grad_scale = 1.0 / math.sqrt(row_count * devices)
    return (
        ret_rows[slot_index],
        ret_grads[slot_index],
        grad_sums[0] * grad_scale,
        grad_sums[1] * grad_scale,
    )


def solution(mesh):
    in_specs = (P(("sx", "sy"), None), P(("sx", "sy"), None), P(("sx", "sy")), P(), P())
    out_specs = (P(("sx", "sy"), None), P(("sx", "sy"), None), P(), P())
    return jax.shard_map(
        on_device, mesh=mesh, in_specs=in_specs, out_specs=out_specs, check_vma=False
    )
```

profile of v0, /device:TPU:1, one launch (start us, length us, event | category | flops | bytes accessed | tf_op | source)
XLA Modules:
  0.0 736.6 jit_solution(12952684937199685522)
XLA Ops:
  7.2 5.1 sort.17
  13.2 4.5 gather_fusion
  18.6 4.3 scatter_custom_fusion
  22.9 4.3 scatter_custom_fusion.1
  27.9 11.5 %all-to-all-start = ((s32[128,16,1]{1,2,0:T(1,128)}), s32[128,16,1]{1,2,0:T(1,128)S(1)}, u32[]{:S(2)}, u32[]{:S(2)}) async-start(s32[128,16,1]{1,2,0:T(1,128)} %bitcast.6), calls=%async_computation | async-start | bytes 131072 | tf_op jit(solution)/shard_map/all_to_all | solution.py:104
  39.4 6.8 scatter_custom_fusion.2
  49.8 6.8 all-to-all-start.1
  56.6 6.8 scatter_custom_fusion.4
  63.4 17.3 %all-to-all-done.1 = bf16[128,16,384]{2,1,0:T(8,128)(2,1)S(1)} async-done(((bf16[128,16,384]{2,1,0:T(8,128)(2,1)}), bf16[128,16,384]{2,1,0:T(8,128)(2,1)S(1)}, u32[]{:S(2)}, u32[]{:S(2)}) %all-to-all-start.1) | async-done | bytes 1572896 | tf_op jit(solution)/shard_map/all_to_all | solution.py:102
  81.8 4.9 all-to-all-start.2
  89.6 9.9 %scatter_custom_fusion.3 = bf16[1024,384]{1,0:T(8,128)(2,1)S(1)} fusion(s32[2048]{0:T(1024)} %bitcast.80, bf16[2048,384]{1,0:T(8,128)(2,1)} %bitcast.76, bf16[]{:T(256)} %constant.129.clone.1), kind=kCustom, calls=%fused_computation.78 | custom fusion | bytes 786944 | tf_op jit(solution)/shard_map/scatter | solution.py:107
  100.9 10.0 %all-to-all-done.2 = bf16[128,16,384]{2,1,0:T(8,128)(2,1)S(1)} async-done(((bf16[128,16,384]{2,1,0:T(8,128)(2,1)}), bf16[128,16,384]{2,1,0:T(8,128)(2,1)S(1)}, u32[]{:S(2)}, u32[]{:S(2)}) %all-to-all-start.2) | async-done | bytes 1572896 | tf_op jit(solution)/shard_map/all_to_all | solution.py:103
  112.1 9.9 %scatter_custom_fusion.5 = bf16[1024,384]{1,0:T(8,128)(2,1)S(1)} fusion(s32[2048]{0:T(1024)} %bitcast.81, bf16[2048,384]{1,0:T(8,128)(2,1)} %bitcast.75, bf16[]{:T(256)} %constant.129.clone.1), kind=kCustom, calls=%fused_computation.76 | custom fusion | bytes 786944 | tf_op jit(solution)/shard_map/scatter | solution.py:110
  122.7 3.7 convolution_convert_fusion.4
  126.9 391.0 %while.32 = (s32[]{:T(128)}, bf16[24,1024,16]{1,2,0:T(8,128)(2,1)}, bf16[24,1024,16]{1,2,0:T(8,128)(2,1)}, bf16[24,1024,16]{1,2,0:T(8,128)(2,1)}, bf16[24,1024,1...) while((s32[]{:T(128)}, bf16[24,1024,16]{1,2,0:T(8,128)(2,1)}, ...), condition=%wide.region_16.17_spmd, body=%wide.region_12.16_spmd.sunk | while | flops 227603472 | bytes 42127728 | solution.py:59
  519.7 9.0 %gather_fusion.1 = bf16[2048,384]{1,0:T(8,128)(2,1)} fusion(bf16[1024,384]{1,0:T(8,128)(2,1)S(1)} %fusion.41, s32[2048]{0:T(1024)S(1)} %broadcast_clamp_fusion), kind=kCustom, calls=%fused_computation.1 | custom fusion | bytes 3153920 | tf_op jit(solution)/shard_map/gather | solution.py:131
  528.8 5.0 all-to-all-start.3
  534.1 3.7 fusion.62
  543.8 3.9 fusion.42
  551.8 9.0 %gather_fusion.3 = bf16[2048,384]{1,0:T(8,128)(2,1)} fusion(bf16[1024,384]{1,0:T(8,128)(2,1)S(1)} %fusion.39, s32[2048]{0:T(1024)S(1)} %broadcast_clamp_fusion), kind=kCustom, calls=%fused_computation.3 | custom fusion | bytes 3153920 | tf_op jit(solution)/shard_map/gather | solution.py:132
  560.8 10.3 %all-to-all-start.4 = ((bf16[128,16,384]{2,1,0:T(8,128)(2,1)}), bf16[128,16,384]{2,1,0:T(8,128)(2,1)}, u32[]{:S(2)}, u32[]{:S(2)}) async-start(bf16[128,16,384]{2,1,0:T(8,128)(2,1)} %bitcast.74), calls=%async_computation.4 | async-start | bytes 3145728 | tf_op jit(solution)/shard_map/all_to_all | solution.py:135
  571.1 142.4 %all-reduce.3.cloned.1.call-done = (f32[384,1152]{1,0:T(8,128)}, f32[384,384]{1,0:T(8,128)}) async-done(((f32[384,1152]{1,0:T(8,128)}, f32[384,384]{1,0:T(8,128)}), (f32[384,1152]{1,0:T(8,128)}, f32[384,384]{1,0:T(8,128)})) %all-reduce.3.cloned.1.call-update) | async-done | bytes 2359312 | tf_op jit(solution)/shard_map/psum | solution.py:137
  718.3 5.0 gather_fusion.2
  723.3 6.5 gather_fusion.4
  (284 shorter events, 404.8 us)
Async XLA Ops:
  7.2 115.5 %copy-start = (bf16[384,1152]{1,0:T(8,128)(2,1)S(1)}, bf16[384,1152]{1,0:T(8,128)(2,1)}, u32[]{:S(2)}) copy-start(bf16[384,1152]{1,0:T(8,128)(2,1)} %param.10) | copy-start | bytes 2654212
  27.9 21.2 %all-to-all-start = ((s32[128,16,1]{1,2,0:T(1,128)}), s32[128,16,1]{1,2,0:T(1,128)S(1)}, u32[]{:S(2)}, u32[]{:S(2)}) async-start(s32[128,16,1]{1,2,0:T(1,128)} %bitcast.6), calls=%async_computation | async-start | bytes 131072 | tf_op jit(solution)/shard_map/all_to_all | solution.py:104
  49.1 0.6 copy-start.9
  49.8 30.9 %all-to-all-start.1 = ((bf16[128,16,384]{2,1,0:T(8,128)(2,1)}), bf16[128,16,384]{2,1,0:T(8,128)(2,1)S(1)}, u32[]{:S(2)}, u32[]{:S(2)}) async-start(bf16[128,16,384]{2,1,0:T(8,128)(2,1)} %bitcast.8), calls=%async_computation.1 | async-start | bytes 3145728 | tf_op jit(solution)/shard_map/all_to_all | solution.py:102
  80.7 1.1 copy-start.7
  81.8 29.1 %all-to-all-start.2 = ((bf16[128,16,384]{2,1,0:T(8,128)(2,1)}), bf16[128,16,384]{2,1,0:T(8,128)(2,1)S(1)}, u32[]{:S(2)}, u32[]{:S(2)}) async-start(bf16[128,16,384]{2,1,0:T(8,128)(2,1)} %bitcast.10), calls=%async_computation.2 | async-start | bytes 3145728 | tf_op jit(solution)/shard_map/all_to_all | solution.py:103
  86.7 35.3 %copy-start.8 = (bf16[384,384]{1,0:T(8,128)(2,1)S(1)}, bf16[384,384]{1,0:T(8,128)(2,1)}, u32[]{:S(2)}) copy-start(bf16[384,384]{1,0:T(8,128)(2,1)} %param.11) | copy-start | bytes 884740
  99.6 418.3 %copy-start.1 = (bf16[1024,384]{1,0:T(8,128)(2,1)}, bf16[1024,384]{1,0:T(8,128)(2,1)S(1)}, u32[]{:S(2)}) copy-start(bf16[1024,384]{1,0:T(8,128)(2,1)S(1)} %scatter_custom_fusion.3) | copy-start | bytes 2359300
  110.9 1.1 copy-start.6
  122.0 4.3 copy-start.5
  528.8 5.3 copy-start.11
  528.8 32.0 %all-to-all-start.3 = ((bf16[128,16,384]{2,1,0:T(8,128)(2,1)}), bf16[128,16,384]{2,1,0:T(8,128)(2,1)S(1)}, u32[]{:S(2)}, u32[]{:S(2)}) async-start(bf16[128,16,384]{2,1,0:T(8,128)(2,1)} %bitcast.73), calls=%async_computation.3 | async-start | bytes 3145728 | tf_op jit(solution)/shard_map/all_to_all | solution.py:134
  533.8 179.7 %all-reduce.3.cloned.1.call-start = ((), (), s32[]{:S(2)}) async-start(), calls=%async_computation.5 | async-start | bytes 4718592 | tf_op jit(solution)/shard_map/psum | solution.py:137
  537.8 6.0 copy-start.2
  537.8 6.0 copy-start.10
  540.9 2.9 copy-start.12
  540.9 2.9 copy-start.13
  547.8 2.1 copy-start.3
  547.8 2.1 copy-start.4
  560.8 162.5 %all-to-all-start.4 = ((bf16[128,16,384]{2,1,0:T(8,128)(2,1)}), bf16[128,16,384]{2,1,0:T(8,128)(2,1)}, u32[]{:S(2)}, u32[]{:S(2)}) async-start(bf16[128,16,384]{2,1,0:T(8,128)(2,1)} %bitcast.74), calls=%async_computation.4 | async-start | bytes 3145728 | tf_op jit(solution)/shard_map/all_to_all | solution.py:135
Sparse Core Ops, SparseCore 0:
  547.9 165.5 all-reduce.2
where the time goes:
time: 741 us; the launch traced here: 737 us
  matrix products  314 us (42%)
  waiting for transfers between devices  173 us (23%)
  local copies, waits for them, and re-layouts  114 us (15%)
  other arithmetic  66.6 us (9%)
  starting transfers between devices  38.8 us (5%)
  loops' own time  16.7 us (2%)
  between operations  14.4 us (2%)
    dot_general x100, matrix products, contract(): lax.dot_general(left_op, right_op, (((left_dim,), (right_dim,)), ((), ())...  199 us
    psum x1, waiting for transfers between devices, on_device(): grad_sums = lax.psum((grad_terms[0], grad_terms[1]), ('sx', 'sy'))  142 us
    dot_general x24, matrix products, head_pass(): jnp.dot(prob_low, value_rows, preferred_element_type=jnp.float32)  59.7 us
    dot_general x24, matrix products, head_pass(): jnp.dot(dscores, key_rows, preferred_element_type=jnp.float32)  49.5 us
    convert_element_type x24, other arithmetic, head_pass(): dscores = (prob_full * (dprobs - jnp.sum(dprobs * prob_full, axis=1, keep...  30.2 us
    dynamic_slice x24, local copies, waits for them, and re-layouts, patch_pass(): heads_out = lax.map(one_head, jnp.arange(head_count, dtype=jnp.int32))  29.7 us
    scatter x2, local copies, waits for them, and re-layouts, on_device(): jnp.zeros((row_count, feat_width), jnp.bfloat16).at[got_place]  19.9 us
    reduce_sum x24, other arithmetic, head_pass(): prob_full = shifted / jnp.sum(shifted, axis=1, keepdims=True)  17.5 us
  transfers between devices with their start and end apart: 6, of which 4 were waited for; matrix products, arithmetic and copies ran while one was open for 9% of the time, Pallas kernels for 0%

commit v1 on v0

--- a/solution.py
+++ b/solution.py
@@ -134,7 +134,7 @@
         lax.all_to_all(back_rows, ("sx", "sy"), split_axis=0, concat_axis=0, tiled=True),
         lax.all_to_all(back_grads, ("sx", "sy"), split_axis=0, concat_axis=0, tiled=True),
     )
-    grad_sums = lax.psum((grad_terms[0], grad_terms[1]), ("sx", "sy"))
+    grad_sums = lax.psum(lax.psum((grad_terms[0], grad_terms[1]), "sy"), "sx")
     grad_scale = 1.0 / math.sqrt(row_count * devices)
     return (
         ret_rows[slot_index],

time: 741 us -> 706 us (0.953)
  local copies, waits for them, and re-layouts: 114 us -> 98.8 us
  waiting for transfers between devices: 173 us -> 159 us
    psum x1 -> x2, waiting for transfers between devices: 142 us -> 124 us  [on_device(): grad_sums = lax.psum(lax.psum((grad_terms[0], grad_terms[1]), 'sy'), 'sx')]
    dynamic_slice x24, local copies, waits for them, and re-layouts: 29.7 us -> 14 us  [patch_pass(): heads_out = lax.map(one_head, jnp.arange(head_count, dtype=jnp.int32))]
  transfers between devices with their start and end apart: 6 -> 7, of which waited for: 4 -> 6; matrix products, arithmetic and copies ran while one was open for 9% -> 10% of each run, Pallas kernels for 0% -> 0%
where the time goes in v1:
time: 706 us; the launch traced here: 700 us
  matrix products  312 us (44%)
  waiting for transfers between devices  159 us (23%)
  local copies, waits for them, and re-layouts  98.8 us (14%)
  other arithmetic  65 us (9%)
  starting transfers between devices  34.5 us (5%)
  loops' own time  16.7 us (2%)
  between operations  14.4 us (2%)
    dot_general x100, matrix products, contract(): lax.dot_general(left_op, right_op, (((left_dim,), (right_dim,)), ((), ())...  199 us
    psum x2, waiting for transfers between devices, on_device(): grad_sums = lax.psum(lax.psum((grad_terms[0], grad_terms[1]), 'sy'), 'sx')  124 us
    dot_general x24, matrix products, head_pass(): jnp.dot(prob_low, value_rows, preferred_element_type=jnp.float32)  59.7 us
    dot_general x24, matrix products, head_pass(): jnp.dot(dscores, key_rows, preferred_element_type=jnp.float32)  49.5 us
    convert_element_type x24, other arithmetic, head_pass(): dscores = (prob_full * (dprobs - jnp.sum(dprobs * prob_full, axis=1, keep...  30.1 us
    scatter x2, local copies, waits for them, and re-layouts, on_device(): jnp.zeros((row_count, feat_width), jnp.bfloat16).at[got_place]  19.9 us
    reduce_sum x24, other arithmetic, head_pass(): prob_full = shifted / jnp.sum(shifted, axis=1, keepdims=True)  17.5 us
    all_to_all x1, waiting for transfers between devices, on_device(): lax.all_to_all(send_rows, ('sx', 'sy'), split_axis=0, concat_axis=0, tile...  17.3 us
  transfers between devices with their start and end apart: 7, of which 6 were waited for; matrix products, arithmetic and copies ran while one was open for 10% of the time, Pallas kernels for 0%

profile of v1, /device:TPU:1, one launch (start us, length us, event | category | flops | bytes accessed | tf_op | source)
XLA Modules:
  0.0 700.3 jit_solution(6472149889551264150)
XLA Ops:
  7.2 5.1 sort.17
  13.2 4.5 gather_fusion
  18.6 4.3 scatter_custom_fusion
  22.9 4.3 scatter_custom_fusion.1
  27.9 11.5 %all-to-all-start = ((s32[128,16,1]{1,2,0:T(1,128)}), s32[128,16,1]{1,2,0:T(1,128)S(1)}, u32[]{:S(2)}, u32[]{:S(2)}) async-start(s32[128,16,1]{1,2,0:T(1,128)} %bitcast.6), calls=%async_computation | async-start | bytes 131072 | tf_op jit(solution)/shard_map/all_to_all | solution.py:104
  39.4 6.8 scatter_custom_fusion.2
  49.8 6.8 all-to-all-start.1
  56.6 6.8 scatter_custom_fusion.4
  63.4 17.3 %all-to-all-done.1 = bf16[128,16,384]{2,1,0:T(8,128)(2,1)S(1)} async-done(((bf16[128,16,384]{2,1,0:T(8,128)(2,1)}), bf16[128,16,384]{2,1,0:T(8,128)(2,1)S(1)}, u32[]{:S(2)}, u32[]{:S(2)}) %all-to-all-start.1) | async-done | bytes 1572896 | tf_op jit(solution)/shard_map/all_to_all | solution.py:102
  81.8 4.9 all-to-all-start.2
  89.9 9.9 %scatter_custom_fusion.3 = bf16[1024,384]{1,0:T(8,128)(2,1)S(1)} fusion(s32[2048]{0:T(1024)} %bitcast.80, bf16[2048,384]{1,0:T(8,128)(2,1)} %bitcast.76, bf16[]{:T(256)} %constant.129.clone.1), kind=kCustom, calls=%fused_computation.78 | custom fusion | bytes 786944 | tf_op jit(solution)/shard_map/scatter | solution.py:107
  100.5 10.4 %all-to-all-done.2 = bf16[128,16,384]{2,1,0:T(8,128)(2,1)S(1)} async-done(((bf16[128,16,384]{2,1,0:T(8,128)(2,1)}), bf16[128,16,384]{2,1,0:T(8,128)(2,1)S(1)}, u32[]{:S(2)}, u32[]{:S(2)}) %all-to-all-start.2) | async-done | bytes 1572896 | tf_op jit(solution)/shard_map/all_to_all | solution.py:103
  112.1 9.9 %scatter_custom_fusion.5 = bf16[1024,384]{1,0:T(8,128)(2,1)S(1)} fusion(s32[2048]{0:T(1024)} %bitcast.81, bf16[2048,384]{1,0:T(8,128)(2,1)} %bitcast.75, bf16[]{:T(256)} %constant.129.clone.1), kind=kCustom, calls=%fused_computation.76 | custom fusion | bytes 786944 | tf_op jit(solution)/shard_map/scatter | solution.py:110
  125.7 375.3 %while.32 = (s32[]{:T(128)}, bf16[24,1024,16]{1,2,0:T(8,128)(2,1)}, bf16[24,1024,16]{1,2,0:T(8,128)(2,1)}, bf16[24,1024,16]{1,2,0:T(8,128)(2,1)}, bf16[24,1024,1...) while((s32[]{:T(128)}, bf16[24,1024,16]{1,2,0:T(8,128)(2,1)}, ...), condition=%wide.region_16.17_spmd, body=%wide.region_12.16_spmd.sunk | while | flops 227603472 | bytes 42127728 | solution.py:59
  503.7 3.9 fusion.42
  509.4 9.0 %gather_fusion.1 = bf16[2048,384]{1,0:T(8,128)(2,1)} fusion(bf16[1024,384]{1,0:T(8,128)(2,1)S(1)} %fusion.41, s32[2048]{0:T(1024)S(1)} %broadcast_clamp_fusion), kind=kCustom, calls=%fused_computation.1 | custom fusion | bytes 3153920 | tf_op jit(solution)/shard_map/gather | solution.py:131
  518.5 5.0 all-to-all-start.3
  534.4 9.0 %gather_fusion.3 = bf16[2048,384]{1,0:T(8,128)(2,1)} fusion(bf16[1024,384]{1,0:T(8,128)(2,1)S(1)} %fusion.39, s32[2048]{0:T(1024)S(1)} %broadcast_clamp_fusion), kind=kCustom, calls=%fused_computation.3 | custom fusion | bytes 3153920 | tf_op jit(solution)/shard_map/gather | solution.py:132
  543.4 4.3 all-to-all-done.3
  547.7 6.0 all-to-all-start.4
  553.8 68.0 %all-reduce.5.cloned.1.call-done = (f32[384,1152]{1,0:T(8,128)}, f32[384,384]{1,0:T(8,128)}) async-done(((f32[384,1152]{1,0:T(8,128)}, f32[384,384]{1,0:T(8,128)}), (f32[384,1152]{1,0:T(8,128)}, f32[384,384]{1,0:T(8,128)})) %all-reduce.5.cloned.1.call-update) | async-done | bytes 2359312 | tf_op jit(solution)/shard_map/psum | solution.py:137
  621.8 5.0 gather_fusion.2
  626.8 6.5 gather_fusion.4
  633.3 56.4 %all-reduce.7.cloned.1.call-done = (f32[384,1152]{1,0:T(8,128)}, f32[384,384]{1,0:T(8,128)}) async-done(((f32[384,1152]{1,0:T(8,128)}, f32[384,384]{1,0:T(8,128)}), (f32[384,1152]{1,0:T(8,128)}, f32[384,384]{1,0:T(8,128)})) %all-reduce.7.cloned.1.call-update) | async-done | bytes 2359312 | tf_op jit(solution)/shard_map/psum | solution.py:137
  (295 shorter events, 393.4 us)
Async XLA Ops:
  7.2 115.5 %copy-start = (bf16[384,1152]{1,0:T(8,128)(2,1)S(1)}, bf16[384,1152]{1,0:T(8,128)(2,1)}, u32[]{:S(2)}) copy-start(bf16[384,1152]{1,0:T(8,128)(2,1)} %param.10) | copy-start | bytes 2654212
  27.9 21.2 %all-to-all-start = ((s32[128,16,1]{1,2,0:T(1,128)}), s32[128,16,1]{1,2,0:T(1,128)S(1)}, u32[]{:S(2)}, u32[]{:S(2)}) async-start(s32[128,16,1]{1,2,0:T(1,128)} %bitcast.6), calls=%async_computation | async-start | bytes 131072 | tf_op jit(solution)/shard_map/all_to_all | solution.py:104
  49.8 30.9 %all-to-all-start.1 = ((bf16[128,16,384]{2,1,0:T(8,128)(2,1)}), bf16[128,16,384]{2,1,0:T(8,128)(2,1)S(1)}, u32[]{:S(2)}, u32[]{:S(2)}) async-start(bf16[128,16,384]{2,1,0:T(8,128)(2,1)} %bitcast.8), calls=%async_computation.1 | async-start | bytes 3145728 | tf_op jit(solution)/shard_map/all_to_all | solution.py:102
  80.7 1.1 copy-start.7
  81.8 29.1 %all-to-all-start.2 = ((bf16[128,16,384]{2,1,0:T(8,128)(2,1)}), bf16[128,16,384]{2,1,0:T(8,128)(2,1)S(1)}, u32[]{:S(2)}, u32[]{:S(2)}) async-start(bf16[128,16,384]{2,1,0:T(8,128)(2,1)} %bitcast.10), calls=%async_computation.2 | async-start | bytes 3145728 | tf_op jit(solution)/shard_map/all_to_all | solution.py:103
  86.7 35.3 %copy-start.10 = (bf16[384,384]{1,0:T(8,128)(2,1)S(1)}, bf16[384,384]{1,0:T(8,128)(2,1)}, u32[]{:S(2)}) copy-start(bf16[384,384]{1,0:T(8,128)(2,1)} %param.11) | copy-start | bytes 884740
  86.7 535.1 %all-reduce.5.cloned.1.call-start = ((), (), s32[]{:S(2)}) async-start(), calls=%async_computation.5 | async-start | bytes 4718592 | tf_op jit(solution)/shard_map/psum | solution.py:137
  99.8 408.5 %copy-start.1 = (bf16[1024,384]{1,0:T(8,128)(2,1)}, bf16[1024,384]{1,0:T(8,128)(2,1)S(1)}, u32[]{:S(2)}) copy-start(bf16[1024,384]{1,0:T(8,128)(2,1)S(1)} %scatter_custom_fusion.3) | copy-start | bytes 2359300
  100.5 403.1 %copy-start.12 = (f32[1024]{0:T(1024)}, f32[1024]{0:T(1024)S(1)}, u32[]{:S(2)}) copy-start(f32[1024]{0:T(1024)S(1)} %add_rsqrt_fusion) | copy-start | bytes 12292
  110.9 1.1 copy-start.6
  122.0 379.0 %copy-start.5 = (bf16[1024,384]{1,0:T(8,128)(2,1)}, bf16[1024,384]{1,0:T(8,128)(2,1)S(1)}, u32[]{:S(2)}) copy-start(bf16[1024,384]{1,0:T(8,128)(2,1)S(1)} %scatter_custom_fusion.5) | copy-start | bytes 2359300
  501.0 2.6 copy-start.15
  501.0 2.7 copy-start.17
  507.6 0.7 copy-start.14
  507.6 1.1 copy-start.8
  518.5 5.0 copy-start.16
  518.5 29.2 %all-to-all-start.3 = ((bf16[128,16,384]{2,1,0:T(8,128)(2,1)}), bf16[128,16,384]{2,1,0:T(8,128)(2,1)S(1)}, u32[]{:S(2)}, u32[]{:S(2)}) async-start(bf16[128,16,384]{2,1,0:T(8,128)(2,1)} %bitcast.74), calls=%async_computation.3 | async-start | bytes 3145728 | tf_op jit(solution)/shard_map/all_to_all | solution.py:134
  527.3 3.1 copy-start.2
  527.3 3.1 copy-start.13
  530.4 2.1 copy-start.3
  530.4 2.1 copy-start.4
  547.7 79.1 %all-to-all-start.4 = ((bf16[128,16,384]{2,1,0:T(8,128)(2,1)}), bf16[128,16,384]{2,1,0:T(8,128)(2,1)}, u32[]{:S(2)}, u32[]{:S(2)}) async-start(bf16[128,16,384]{2,1,0:T(8,128)(2,1)} %bitcast.73), calls=%async_computation.4 | async-start | bytes 3145728 | tf_op jit(solution)/shard_map/all_to_all | solution.py:135
  553.8 136.0 %all-reduce.7.cloned.1.call-start = ((), (), s32[]{:S(2)}) async-start(), calls=%async_computation.6 | async-start | bytes 4718592 | tf_op jit(solution)/shard_map/psum | solution.py:137
  689.7 2.9 copy-start.9
  (1 other events, 0.6 us)
Sparse Core Ops, SparseCore 0:
  507.7 114.0 all-reduce.4
  624.3 65.3 all-reduce.6
